TPU v7x, 32 devices: a whole 2x2x4 slice. The times are simulated.
32 devices in a mesh: domain: 2 (over x), fsdp: 16 (over z, y, core).
Axes of the slice: x: 2, y: 2, z: 4, core: 2. Of those that a mesh axis runs over, the one named last changes fastest.
Arguments:
- gradients: bfloat16 [2, 4, 4096, 512], P('domain', None, 'fsdp')
- row_counts: int32 [4], replicated, may hold values from 2048 to 4096, as said below
- domain_ids: int32 [2], replicated, may hold values from 0 to 7
- domain_weights: float32 [8], replicated, may hold values from 0.2 to 2
Outputs:
- updates: float32 [4, 4096, 512], P('domain', 'fsdp')
- new_weights: float32 [8], replicated
Inputs may be any that keep to these rules, and one draw needn't show every extreme that they name: `row_counts`: each matrix has 4096 or 2048 rows, and both counts occur.
All inputs are finite; a program needn't handle non-finite values.
Results may differ from a plain program's by a relative error of at most 0.0071.
Values may be sent and summed in bfloat16 or wider, within the bound.
No kernel may reach another device: no remote copies, remote signals or barrier semaphores. Data moves between devices by JAX's collectives and lax.ppermute only.
A program may use at most 64 MiB of HBM per device.

v0:
```python
import math
import jax
import jax.numpy as jnp
from jax import lax
from jax.sharding import PartitionSpec as P

NS_ITERS = 3
OWNERS = 8
COEF_A = 3.4445
COEF_B = -4.775
COEF_C = 2.0315
MUON_SCALE = 0.2
ETA = 4.0


def partner(shard, axis, stride):
    return lax.ppermute(shard, axis, [(i, i ^ 1 << stride) for i in range(lax.axis_size(axis))])


def group_mixing(domain_ids, domain_weights, kind_count):
    weight_share = domain_weights / jnp.sum(domain_weights)
    onehot = (domain_ids[:, None] == jnp.arange(kind_count, dtype=jnp.int32)[None, :]).astype(
        jnp.float32
    )
    counts = jnp.sum(onehot, axis=0)
    per_member = weight_share / jnp.maximum(counts, 1.0)
    group_mix = jnp.sum(onehot * per_member[None, :], axis=1)
    return (weight_share, onehot, counts, group_mix)


def summed_gram(iterate):
    gram_total = lax.dot_general(
        iterate, iterate, (((0,), (0,)), ((), ())), preferred_element_type=jnp.float32
    )
    for bit_pos in range(OWNERS.bit_length() - 1):
        gram_total = gram_total + partner(gram_total, "fsdp", bit_pos)
    return gram_total


def newton_steps(iterate):
    for repeat in range(NS_ITERS):
        gram_full = lax.optimization_barrier(summed_gram(iterate).astype(jnp.bfloat16))
        square = jnp.dot(gram_full, gram_full, preferred_element_type=jnp.float32)
        poly_term = (COEF_B * gram_full.astype(jnp.float32) + COEF_C * square).astype(jnp.bfloat16)
        iterate = lax.optimization_barrier(
            (
                COEF_A * iterate.astype(jnp.float32)
                + jnp.dot(iterate, poly_term, preferred_element_type=jnp.float32)
            ).astype(jnp.bfloat16)
        )
    return iterate


def share_scores(aligned, squares, norm_slots):
    return lax.psum((aligned, squares, norm_slots), ("domain", "fsdp"))


def body(gradients, row_counts, domain_ids, domain_weights):
    groups = lax.axis_size("domain")
    shards = lax.axis_size("fsdp")
    matrices = row_counts.shape[0]
    rows_src = gradients.shape[2]
    columns = gradients.shape[3]
    per_domain = matrices // groups
    sub_rows = rows_src // OWNERS
    own_rows = shards * sub_rows
    full_rows = rows_src * shards
    domain_pos = lax.axis_index("domain")
    shard_pos = lax.axis_index("fsdp")
    weight_share, onehot, counts, group_mix = group_mixing(
        domain_ids, domain_weights, domain_weights.shape[0]
    )
    blocks = lax.all_to_all(
        gradients.reshape(1, groups, per_domain, rows_src, columns),
        "domain",
        split_axis=1,
        concat_axis=0,
        tiled=True,
    )
    blocks = blocks.reshape(groups, per_domain, rows_src, columns)
    global_rows = shard_pos * rows_src + jnp.arange(rows_src, dtype=jnp.int32)
    limits = lax.dynamic_slice_in_dim(row_counts, domain_pos * per_domain, per_domain, 0)
    row_mask = (global_rows[None, :] < limits[:, None])[None, :, :, None]
    masked = jnp.where(row_mask, blocks.astype(jnp.float32), jnp.zeros((), jnp.float32))
    combined = jnp.sum(group_mix[:, None, None, None] * masked, axis=0)
    aligned = jnp.sum(masked * combined[None], axis=(1, 2, 3))
    squares = jnp.sum(masked * masked, axis=(1, 2, 3))
    block_squares = jnp.sum(combined * combined, axis=(1, 2))
    norm_slots = lax.dynamic_update_slice_in_dim(
        jnp.zeros((matrices,), jnp.float32), block_squares, domain_pos * per_domain, 0
    )
    aligned, squares, norm_slots = share_scores(aligned, squares, norm_slots)
    frob_norm = (
        jnp.sqrt(lax.dynamic_slice_in_dim(norm_slots, domain_pos * per_domain, per_domain, 0))
        + 1e-07
    )
    scaled = (combined / frob_norm[:, None, None]).astype(jnp.bfloat16)
    scaled = scaled.reshape(shards, 1, sub_rows, columns)
    start_rows = lax.all_to_all(scaled, "fsdp", split_axis=0, concat_axis=1, tiled=True)
    start_rows = lax.optimization_barrier(start_rows.reshape(own_rows, columns))
    finished = newton_steps(start_rows)
    returned = lax.all_to_all(
        finished.reshape(1, shards, sub_rows, columns),
        "fsdp",
        split_axis=1,
        concat_axis=0,
        tiled=True,
    )
    returned = returned.reshape(per_domain, rows_src, columns)
    updates = returned.astype(jnp.float32) * (MUON_SCALE * math.sqrt(full_rows))
    total_sq = jnp.sum(norm_slots)
    cosine = aligned / (jnp.sqrt(squares) * jnp.sqrt(total_sq) + 1e-06)
    score = jnp.sum(onehot * cosine[:, None], axis=0) / jnp.maximum(counts, 1.0)
    raised = weight_share * jnp.exp(ETA * score)
    return (updates, raised / jnp.sum(raised))


def solution(mesh):
    placed = (P("domain", None, "fsdp", None), P(), P(), P())
    return jax.shard_map(
        body,
        mesh=mesh,
        in_specs=placed,
        out_specs=(P("domain", "fsdp", None), P()),
        check_vma=False,
    )
```

profile of v0, /device:TPU:0, one launch (start us, length us, event | category | flops | bytes accessed | tf_op | source)
XLA Modules:
  0.0 265.7 jit_solution(6877497156156330844)
XLA Ops:
  0.7 4.4 %all-to-all-start = ((bf16[1,2,2,256,512]{4,3,2,0,1:T(8,128)(2,1)}), bf16[1,2,2,256,512]{4,3,2,0,1:T(8,128)(2,1)S(1)}, u32[]{:S(2)}, u32[]{:S(2)}) async-start(bf16[1,2,2,256,512]{4,3,2,0,1:T(8,128)(2,1)} %bitcast.31), calls=%async_computation | async-start | bytes 2097152 | tf_op jit(solution)/shard_map/all_to_all | solution.py:73
  6.7 12.7 %all-to-all-done = bf16[1,2,2,256,512]{4,3,2,0,1:T(8,128)(2,1)S(1)} async-done(((bf16[1,2,2,256,512]{4,3,2,0,1:T(8,128)(2,1)}), bf16[1,2,2,256,512]{4,3,2,0,1:T(8,128)(2,1)S(1)}, u32[]{:S(2)}, u32[]{:S(2)}) %all-to-all-start) | async-done | bytes 1048608 | tf_op jit(solution)/shard_map/all_to_all | solution.py:73
  20.9 39.8 %all-reduce = (f32[4]{0:T(128)S(1)}, f32[2]{0:T(128)S(1)}, f32[2]{0:T(128)S(1)}) all-reduce(f32[4]{0:T(128)S(1)} %dynamic_update_slice.3, f32[2]{0:T(128)S(1)} %get-tuple-element.3, f32[2]{0:T(128)S(1)} %get-tuple-element.2), channel_id=1, replica_groups=mesh['domain'=2,'fsdp'=16] {'domain','fsdp'}, use_global_device_ids=true, to_apply=%region_5.6 | all-reduce | flops 8 | bytes 64 | tf_op jit(solution)/shard_map/psum | solution.py:55
  62.4 19.5 %all_to_all.12 = bf16[16,1,32,512]{3,2,1,0:T(8,128)(2,1)S(1)} all-to-all(bf16[16,1,32,512]{3,2,1,0:T(8,128)(2,1)S(1)} %divide_convert_fusion), channel_id=1, replica_groups=mesh['domain'=2,'fsdp'=16] {'fsdp'}, dimensions={0} | all-to-all | bytes 1048576 | tf_op jit(solution)/shard_map/all_to_all | solution.py:99
  82.6 2.5 collective-permute-done
  86.4 24.2 %collective-permute-done.1 = f32[512,512]{1,0:T(8,128)S(1)} collective-permute-done((f32[512,512]{1,0:T(8,128)S(1)}, f32[512,512]{1,0:T(8,128)S(1)}, u32[]{:S(2)}, u32[]{:S(2)}) %collective-permute-start.1) | collective-permute-done | bytes 1048608 | tf_op jit(solution)/shard_map/ppermute | solution.py:17
  110.8 1.8 collective-permute-start.2
  112.6 22.8 %collective-permute-done.2 = f32[512,512]{1,0:T(8,128)S(1)} collective-permute-done((f32[512,512]{1,0:T(8,128)S(1)}, f32[512,512]{1,0:T(8,128)S(1)}, u32[]{:S(2)}, u32[]{:S(2)}) %collective-permute-start.2) | collective-permute-done | bytes 1048608 | tf_op jit(solution)/shard_map/ppermute | solution.py:17
  137.0 2.6 collective-permute-done.3
  139.9 1.3 collective-permute-start.4
  141.2 23.9 %collective-permute-done.4 = f32[512,512]{1,0:T(8,128)S(1)} collective-permute-done((f32[512,512]{1,0:T(8,128)S(1)}, f32[512,512]{1,0:T(8,128)S(1)}, u32[]{:S(2)}, u32[]{:S(2)}) %collective-permute-start.4) | collective-permute-done | bytes 1048608 | tf_op jit(solution)/shard_map/ppermute | solution.py:17
  165.4 1.8 collective-permute-start.5
  167.2 22.6 %collective-permute-done.5 = f32[512,512]{1,0:T(8,128)S(1)} collective-permute-done((f32[512,512]{1,0:T(8,128)S(1)}, f32[512,512]{1,0:T(8,128)S(1)}, u32[]{:S(2)}, u32[]{:S(2)}) %collective-permute-start.5) | collective-permute-done | bytes 1048608 | tf_op jit(solution)/shard_map/ppermute | solution.py:17
  191.4 2.6 collective-permute-done.6
  194.2 1.3 collective-permute-start.7
  195.6 23.9 %collective-permute-done.7 = f32[512,512]{1,0:T(8,128)S(1)} collective-permute-done((f32[512,512]{1,0:T(8,128)S(1)}, f32[512,512]{1,0:T(8,128)S(1)}, u32[]{:S(2)}, u32[]{:S(2)}) %collective-permute-start.7) | collective-permute-done | bytes 1048608 | tf_op jit(solution)/shard_map/ppermute | solution.py:17
  219.7 1.8 collective-permute-start.8
  221.5 22.6 %collective-permute-done.8 = f32[512,512]{1,0:T(8,128)S(1)} collective-permute-done((f32[512,512]{1,0:T(8,128)S(1)}, f32[512,512]{1,0:T(8,128)S(1)}, u32[]{:S(2)}, u32[]{:S(2)}) %collective-permute-start.8) | collective-permute-done | bytes 1048608 | tf_op jit(solution)/shard_map/ppermute | solution.py:17
  244.4 1.6 fusion.8
  245.9 4.4 %all-to-all-start.2 = ((bf16[1,16,32,512]{3,2,0,1:T(8,128)(2,1)}), bf16[1,16,32,512]{3,2,0,1:T(8,128)(2,1)S(1)}, u32[]{:S(2)}, u32[]{:S(2)}) async-start(bf16[1,16,32,512]{3,2,0,1:T(8,128)(2,1)} %bitcast.5), calls=%async_computation.2 | async-start | bytes 1048576 | tf_op jit(solution)/shard_map/all_to_all | solution.py:102
  250.4 1.3 fusion.21
  251.8 1.2 broadcast_divide_fusion
  253.0 11.6 %all-to-all-done.2 = bf16[1,16,32,512]{3,2,0,1:T(8,128)(2,1)S(1)} async-done(((bf16[1,16,32,512]{3,2,0,1:T(8,128)(2,1)}), bf16[1,16,32,512]{3,2,0,1:T(8,128)(2,1)S(1)}, u32[]{:S(2)}, u32[]{:S(2)}) %all-to-all-start.2) | async-done | bytes 524320 | tf_op jit(solution)/shard_map/all_to_all | solution.py:102
  264.6 1.1 convert_multiply_fusion
  (42 shorter events, 10.6 us)
Async XLA Ops:
  0.6 4.4 %copy-start.2 = (s32[2]{0:T(128)S(1)}, s32[2]{0:T(128)}, u32[]{:S(2)}) copy-start(s32[2]{0:T(128)} %param.6) | copy-start | bytes 28
  0.6 4.5 %copy-start = (f32[8]{0:T(128)S(1)}, f32[8]{0:T(128)}, u32[]{:S(2)}) copy-start(f32[8]{0:T(128)} %param.7) | copy-start | bytes 100
  0.7 5.1 %copy-start.1 = (s32[4]{0:T(128)S(1)}, s32[4]{0:T(128)}, u32[]{:S(2)}) copy-start(s32[4]{0:T(128)} %param.5) | copy-start | bytes 52
  0.7 18.8 %all-to-all-start = ((bf16[1,2,2,256,512]{4,3,2,0,1:T(8,128)(2,1)}), bf16[1,2,2,256,512]{4,3,2,0,1:T(8,128)(2,1)S(1)}, u32[]{:S(2)}, u32[]{:S(2)}) async-start(bf16[1,2,2,256,512]{4,3,2,0,1:T(8,128)(2,1)} %bitcast.31), calls=%async_computation | async-start | bytes 2097152 | tf_op jit(solution)/shard_map/all_to_all | solution.py:73
  82.4 2.7 %collective-permute-start = (f32[512,512]{1,0:T(8,128)S(1)}, f32[512,512]{1,0:T(8,128)S(1)}, u32[]{:S(2)}, u32[]{:S(2)}) collective-permute-start(f32[512,512]{1,0:T(8,128)S(1)} %fusion.22), channel_id=1, source_target_pairs={{0,1},{1,0},{2,3},{3,2},{4,5},{5,4},{6,7},{7,6},{8,9},{9,8},{10,11... | collective-permute-start | bytes 3145736 | tf_op jit(solution)/shard_map/ppermute | solution.py:17
  85.3 25.3 %collective-permute-start.1 = (f32[512,512]{1,0:T(8,128)S(1)}, f32[512,512]{1,0:T(8,128)S(1)}, u32[]{:S(2)}, u32[]{:S(2)}) collective-permute-start(f32[512,512]{1,0:T(8,128)S(1)} %add.76), channel_id=1, source_target_pairs={{0,2},{1,3},{2,0},{3,1},{4,6},{5,7},{6,4},{7,5},{8,10},{9,11},{10,... | collective-permute-start | bytes 3145736 | tf_op jit(solution)/shard_map/ppermute | solution.py:17
  110.8 24.7 %collective-permute-start.2 = (f32[512,512]{1,0:T(8,128)S(1)}, f32[512,512]{1,0:T(8,128)S(1)}, u32[]{:S(2)}, u32[]{:S(2)}) collective-permute-start(f32[512,512]{1,0:T(8,128)S(1)} %add.77), channel_id=1, source_target_pairs={{0,4},{1,5},{2,6},{3,7},{4,0},{5,1},{6,2},{7,3},{8,12},{9,13},{10,... | collective-permute-start | bytes 3145736 | tf_op jit(solution)/shard_map/ppermute | solution.py:17
  137.0 2.7 %collective-permute-start.3 = (f32[512,512]{1,0:T(8,128)S(1)}, f32[512,512]{1,0:T(8,128)S(1)}, u32[]{:S(2)}, u32[]{:S(2)}) collective-permute-start(f32[512,512]{1,0:T(8,128)S(1)} %fusion.23), channel_id=1, source_target_pairs={{0,1},{1,0},{2,3},{3,2},{4,5},{5,4},{6,7},{7,6},{8,9},{9,8},{10,11... | collective-permute-start | bytes 3145736 | tf_op jit(solution)/shard_map/ppermute | solution.py:17
  139.9 25.3 %collective-permute-start.4 = (f32[512,512]{1,0:T(8,128)S(1)}, f32[512,512]{1,0:T(8,128)S(1)}, u32[]{:S(2)}, u32[]{:S(2)}) collective-permute-start(f32[512,512]{1,0:T(8,128)S(1)} %add.81), channel_id=1, source_target_pairs={{0,2},{1,3},{2,0},{3,1},{4,6},{5,7},{6,4},{7,5},{8,10},{9,11},{10,... | collective-permute-start | bytes 3145736 | tf_op jit(solution)/shard_map/ppermute | solution.py:17
  165.4 24.4 %collective-permute-start.5 = (f32[512,512]{1,0:T(8,128)S(1)}, f32[512,512]{1,0:T(8,128)S(1)}, u32[]{:S(2)}, u32[]{:S(2)}) collective-permute-start(f32[512,512]{1,0:T(8,128)S(1)} %add.82), channel_id=1, source_target_pairs={{0,4},{1,5},{2,6},{3,7},{4,0},{5,1},{6,2},{7,3},{8,12},{9,13},{10,... | collective-permute-start | bytes 3145736 | tf_op jit(solution)/shard_map/ppermute | solution.py:17
  191.3 2.7 %collective-permute-start.6 = (f32[512,512]{1,0:T(8,128)S(1)}, f32[512,512]{1,0:T(8,128)S(1)}, u32[]{:S(2)}, u32[]{:S(2)}) collective-permute-start(f32[512,512]{1,0:T(8,128)S(1)} %fusion.24), channel_id=1, source_target_pairs={{0,1},{1,0},{2,3},{3,2},{4,5},{5,4},{6,7},{7,6},{8,9},{9,8},{10,11... | collective-permute-start | bytes 3145736 | tf_op jit(solution)/shard_map/ppermute | solution.py:17
  194.2 25.3 %collective-permute-start.7 = (f32[512,512]{1,0:T(8,128)S(1)}, f32[512,512]{1,0:T(8,128)S(1)}, u32[]{:S(2)}, u32[]{:S(2)}) collective-permute-start(f32[512,512]{1,0:T(8,128)S(1)} %add.86), channel_id=1, source_target_pairs={{0,2},{1,3},{2,0},{3,1},{4,6},{5,7},{6,4},{7,5},{8,10},{9,11},{10,... | collective-permute-start | bytes 3145736 | tf_op jit(solution)/shard_map/ppermute | solution.py:17
  219.7 24.4 %collective-permute-start.8 = (f32[512,512]{1,0:T(8,128)S(1)}, f32[512,512]{1,0:T(8,128)S(1)}, u32[]{:S(2)}, u32[]{:S(2)}) collective-permute-start(f32[512,512]{1,0:T(8,128)S(1)} %add.87), channel_id=1, source_target_pairs={{0,4},{1,5},{2,6},{3,7},{4,0},{5,1},{6,2},{7,3},{8,12},{9,13},{10,... | collective-permute-start | bytes 3145736 | tf_op jit(solution)/shard_map/ppermute | solution.py:17
  245.9 18.7 %all-to-all-start.2 = ((bf16[1,16,32,512]{3,2,0,1:T(8,128)(2,1)}), bf16[1,16,32,512]{3,2,0,1:T(8,128)(2,1)S(1)}, u32[]{:S(2)}, u32[]{:S(2)}) async-start(bf16[1,16,32,512]{3,2,0,1:T(8,128)(2,1)} %bitcast.5), calls=%async_computation.2 | async-start | bytes 1048576 | tf_op jit(solution)/shard_map/all_to_all | solution.py:102
where the time goes:
time: 266 us
  waiting for transfers between devices  172 us (65%)
  blocking collectives  59.3 us (22%)
  starting transfers between devices  18.3 us (7%)
  other arithmetic  9.43 us (4%)
  matrix products  4.55 us (2%)
    ppermute x9, waiting for transfers between devices, partner(): lax.ppermute(shard, axis, [(i, i ^ 1 << stride) for i in range(lax.axis_s...  148 us
    psum x1, blocking collectives, share_scores(): return lax.psum((aligned, squares, norm_slots), ('domain', 'fsdp'))  39.8 us
    all_to_all x1, blocking collectives, body(): lax.all_to_all(scaled, 'fsdp', split_axis=0, concat_axis=1, tiled=True)  19.5 us
    all_to_all x1, waiting for transfers between devices, body(): lax.all_to_all(gradients.reshape(1, groups, per_domain, rows_src, columns...  12.7 us
    all_to_all x1, waiting for transfers between devices, body(): lax.all_to_all(finished.reshape(1, shards, sub_rows, columns), 'fsdp', sp...  11.6 us
    ppermute x9, starting transfers between devices, partner(): lax.ppermute(shard, axis, [(i, i ^ 1 << stride) for i in range(lax.axis_s...  9.5 us
  transfers between devices with their start and end apart: 11, of which 11 were waited for; matrix products, arithmetic and copies ran while one was open for 2% of the time, Pallas kernels for 0%

commit v1 on v0

--- a/solution.py
+++ b/solution.py
@@ -11,6 +11,28 @@
 COEF_C = 2.0315
 MUON_SCALE = 0.2
 ETA = 4.0
+
+
+def cut_along(x, dim, size):
+    before, after = (x.shape[:dim], x.shape[dim + 1 :])
+    return jnp.moveaxis(x.reshape(*before, size, -1, *after), dim, 0)
+
+
+def joined_along(parts, dim):
+    shape = list(parts.shape[1:])
+    shape[dim] *= parts.shape[0]
+    return jnp.moveaxis(parts, 0, dim).reshape(shape)
+
+
+def exchange_in_pairs(x, axis, split_dim, concat_dim):
+    length, index = (lax.axis_size(axis), lax.axis_index(axis))
+    blocks = cut_along(x, split_dim, length)
+    outs = [blocks[index]]
+    for step in range(1, length):
+        sent = blocks[index ^ step]
+        outs.append(lax.ppermute(sent, axis, [(i, i ^ step) for i in range(length)]))
+    blocks = jnp.stack(outs)[index ^ jnp.arange(length)]
+    return joined_along(blocks, concat_dim)
 
 
 def partner(shard, axis, stride):
@@ -96,7 +118,7 @@
     )
     scaled = (combined / frob_norm[:, None, None]).astype(jnp.bfloat16)
     scaled = scaled.reshape(shards, 1, sub_rows, columns)
-    start_rows = lax.all_to_all(scaled, "fsdp", split_axis=0, concat_axis=1, tiled=True)
+    start_rows = exchange_in_pairs(scaled, "fsdp", 0, 1)
     start_rows = lax.optimization_barrier(start_rows.reshape(own_rows, columns))
     finished = newton_steps(start_rows)
     returned = lax.all_to_all(

time: 266 us -> 300 us (1.13)
  waiting for transfers between devices: 172 us -> 214 us
  blocking collectives: 59.3 us -> 39.8 us
  starting transfers between devices: 18.3 us -> 29.3 us
    ppermute x0 -> x15, waiting for transfers between devices: none -> 36.8 us  [exchange_in_pairs(): lax.ppermute(sent, axis, [(i, i ^ step) for i in range(length)])]
    all_to_all x1 -> x0, blocking collectives: 19.5 us -> none  [body(): lax.all_to_all(scaled, 'fsdp', split_axis=0, concat_axis=1, tiled=True)]
    ppermute x0 -> x15, starting transfers between devices: none -> 16.2 us  [exchange_in_pairs(): lax.ppermute(sent, axis, [(i, i ^ step) for i in range(length)])]
    ppermute x9, starting transfers between devices: 9.5 us -> 4.74 us  [partner(): lax.ppermute(shard, axis, [(i, i ^ 1 << stride) for i in range(lax.axis_s...]
    ppermute x9, waiting for transfers between devices: 148 us -> 152 us  [partner(): lax.ppermute(shard, axis, [(i, i ^ 1 << stride) for i in range(lax.axis_s...]
  transfers between devices with their start and end apart: 11 -> 26, of which waited for: 11 -> 21; matrix products, arithmetic and copies ran while one was open for 2% -> 1% of each run, Pallas kernels for 0% -> 0%
where the time goes in v1:
time: 300 us; the launch traced here: 299 us
  waiting for transfers between devices  214 us (71%)
  blocking collectives  39.8 us (13%)
  starting transfers between devices  29.3 us (10%)
  other arithmetic  9.3 us (3%)
  matrix products  4.54 us (2%)
    ppermute x9, waiting for transfers between devices, partner(): lax.ppermute(shard, axis, [(i, i ^ 1 << stride) for i in range(lax.axis_s...  152 us
    psum x1, blocking collectives, share_scores(): return lax.psum((aligned, squares, norm_slots), ('domain', 'fsdp'))  39.8 us
    ppermute x15, waiting for transfers between devices, exchange_in_pairs(): lax.ppermute(sent, axis, [(i, i ^ step) for i in range(length)])  36.8 us
    ppermute x15, starting transfers between devices, exchange_in_pairs(): lax.ppermute(sent, axis, [(i, i ^ step) for i in range(length)])  16.2 us
    all_to_all x1, waiting for transfers between devices, body(): lax.all_to_all(gradients.reshape(1, groups, per_domain, rows_src, columns...  12.7 us
    all_to_all x1, waiting for transfers between devices, body(): lax.all_to_all(finished.reshape(1, shards, sub_rows, columns), 'fsdp', sp...  11.8 us
  transfers between devices with their start and end apart: 26, of which 21 were waited for; matrix products, arithmetic and copies ran while one was open for 1% of the time, Pallas kernels for 0%

profile of v1, /device:TPU:0, one launch (start us, length us, event | category | flops | bytes accessed | tf_op | source)
XLA Modules:
  0.0 299.4 jit_solution(16418024474063414166)
XLA Ops:
  0.7 4.4 %all-to-all-start = ((bf16[1,2,2,256,512]{4,3,2,0,1:T(8,128)(2,1)}), bf16[1,2,2,256,512]{4,3,2,0,1:T(8,128)(2,1)S(1)}, u32[]{:S(2)}, u32[]{:S(2)}) async-start(bf16[1,2,2,256,512]{4,3,2,0,1:T(8,128)(2,1)} %bitcast.94), calls=%async_computation | async-start | bytes 2097152 | tf_op jit(solution)/shard_map/all_to_all | solution.py:95
  6.8 12.7 %all-to-all-done = bf16[1,2,2,256,512]{4,3,2,0,1:T(8,128)(2,1)S(1)} async-done(((bf16[1,2,2,256,512]{4,3,2,0,1:T(8,128)(2,1)}), bf16[1,2,2,256,512]{4,3,2,0,1:T(8,128)(2,1)S(1)}, u32[]{:S(2)}, u32[]{:S(2)}) %all-to-all-start) | async-done | bytes 1048608 | tf_op jit(solution)/shard_map/all_to_all | solution.py:95
  20.9 39.8 %all-reduce = (f32[4]{0:T(128)S(1)}, f32[2]{0:T(128)S(1)}, f32[2]{0:T(128)S(1)}) all-reduce(f32[4]{0:T(128)S(1)} %dynamic_update_slice.3, f32[2]{0:T(128)S(1)} %get-tuple-element.3, f32[2]{0:T(128)S(1)} %get-tuple-element.2), channel_id=1, replica_groups=mesh['domain'=2,'fsdp'=16] {'domain','fsdp'}, use_global_device_ids=true, to_apply=%region_5.6 | all-reduce | flops 8 | bytes 64 | tf_op jit(solution)/shard_map/psum | solution.py:77
  62.6 4.0 %collective-permute-start.14 = (bf16[1,1,32,512]{3,2,1,0:T(8,128)(2,1)S(1)}, bf16[1,1,32,512]{3,2,1,0:T(8,128)(2,1)S(1)}, u32[]{:S(2)}, u32[]{:S(2)}) collective-permute-start(bf16[1,1,32,512]{3,2,1,0:T(8,128)(2,1)S(1)} %get-tuple-element.9), channel_id=1, source_target_pairs={{0,15},{1,14},{2,13},{3,12},{4,11},{5,10},{6,9},{7,8},{8,7},{9,6},... | collective-permute-start | bytes 98312 | tf_op jit(solution)/shard_map/ppermute | solution.py:33
  70.7 2.3 collective-permute-start.1
  78.3 3.9 %collective-permute-done.3 = bf16[1,1,32,512]{3,2,1,0:T(8,128)(2,1)S(1)} collective-permute-done((bf16[1,1,32,512]{3,2,1,0:T(8,128)(2,1)S(1)}, bf16[1,1,32,512]{3,2,1,0:T(8,128)(2,1)S(1)}, u32[]{:S(2)}, u32[]{:S(2)}) %collective-permute-start.3) | collective-permute-done | bytes 32800 | tf_op jit(solution)/shard_map/ppermute | solution.py:33
  82.2 3.3 %collective-permute-done.4 = bf16[1,1,32,512]{3,2,1,0:T(8,128)(2,1)S(1)} collective-permute-done((bf16[1,1,32,512]{3,2,1,0:T(8,128)(2,1)S(1)}, bf16[1,1,32,512]{3,2,1,0:T(8,128)(2,1)S(1)}, u32[]{:S(2)}, u32[]{:S(2)}) %collective-permute-start.4) | collective-permute-done | bytes 32800 | tf_op jit(solution)/shard_map/ppermute | solution.py:33
  87.0 3.3 %collective-permute-done.5 = bf16[1,1,32,512]{3,2,1,0:T(8,128)(2,1)S(1)} collective-permute-done((bf16[1,1,32,512]{3,2,1,0:T(8,128)(2,1)S(1)}, bf16[1,1,32,512]{3,2,1,0:T(8,128)(2,1)S(1)}, u32[]{:S(2)}, u32[]{:S(2)}) %collective-permute-start.5) | collective-permute-done | bytes 32800 | tf_op jit(solution)/shard_map/ppermute | solution.py:33
  90.7 3.9 %collective-permute-done.6 = bf16[1,1,32,512]{3,2,1,0:T(8,128)(2,1)S(1)} collective-permute-done((bf16[1,1,32,512]{3,2,1,0:T(8,128)(2,1)S(1)}, bf16[1,1,32,512]{3,2,1,0:T(8,128)(2,1)S(1)}, u32[]{:S(2)}, u32[]{:S(2)}) %collective-permute-start.6) | collective-permute-done | bytes 32800 | tf_op jit(solution)/shard_map/ppermute | solution.py:33
  95.9 3.8 %collective-permute-done.7 = bf16[1,1,32,512]{3,2,1,0:T(8,128)(2,1)S(1)} collective-permute-done((bf16[1,1,32,512]{3,2,1,0:T(8,128)(2,1)S(1)}, bf16[1,1,32,512]{3,2,1,0:T(8,128)(2,1)S(1)}, u32[]{:S(2)}, u32[]{:S(2)}) %collective-permute-start.7) | collective-permute-done | bytes 32800 | tf_op jit(solution)/shard_map/ppermute | solution.py:33
  99.7 4.7 %collective-permute-done.8 = bf16[1,1,32,512]{3,2,1,0:T(8,128)(2,1)S(1)} collective-permute-done((bf16[1,1,32,512]{3,2,1,0:T(8,128)(2,1)S(1)}, bf16[1,1,32,512]{3,2,1,0:T(8,128)(2,1)S(1)}, u32[]{:S(2)}, u32[]{:S(2)}) %collective-permute-start.8) | collective-permute-done | bytes 32800 | tf_op jit(solution)/shard_map/ppermute | solution.py:33
  106.0 4.1 %collective-permute-done.9 = bf16[1,1,32,512]{3,2,1,0:T(8,128)(2,1)S(1)} collective-permute-done((bf16[1,1,32,512]{3,2,1,0:T(8,128)(2,1)S(1)}, bf16[1,1,32,512]{3,2,1,0:T(8,128)(2,1)S(1)}, u32[]{:S(2)}, u32[]{:S(2)}) %collective-permute-start.9) | collective-permute-done | bytes 32800 | tf_op jit(solution)/shard_map/ppermute | solution.py:33
  110.2 5.4 %collective-permute-done.10 = bf16[1,1,32,512]{3,2,1,0:T(8,128)(2,1)S(1)} collective-permute-done((bf16[1,1,32,512]{3,2,1,0:T(8,128)(2,1)S(1)}, bf16[1,1,32,512]{3,2,1,0:T(8,128)(2,1)S(1)}, u32[]{:S(2)}, u32[]{:S(2)}) %collective-permute-start.10) | collective-permute-done | bytes 32800 | tf_op jit(solution)/shard_map/ppermute | solution.py:33
  116.8 2.6 collective-permute-done.15
  120.9 24.1 %collective-permute-done.16 = f32[512,512]{1,0:T(8,128)S(1)} collective-permute-done((f32[512,512]{1,0:T(8,128)S(1)}, f32[512,512]{1,0:T(8,128)S(1)}, u32[]{:S(2)}, u32[]{:S(2)}) %collective-permute-start.16) | collective-permute-done | bytes 1048608 | tf_op jit(solution)/shard_map/ppermute | solution.py:39
  145.4 24.1 %collective-permute-done.17 = f32[512,512]{1,0:T(8,128)S(1)} collective-permute-done((f32[512,512]{1,0:T(8,128)S(1)}, f32[512,512]{1,0:T(8,128)S(1)}, u32[]{:S(2)}, u32[]{:S(2)}) %collective-permute-start.17) | collective-permute-done | bytes 1048608 | tf_op jit(solution)/shard_map/ppermute | solution.py:39
  171.2 2.6 collective-permute-done.18
  175.2 24.1 %collective-permute-done.19 = f32[512,512]{1,0:T(8,128)S(1)} collective-permute-done((f32[512,512]{1,0:T(8,128)S(1)}, f32[512,512]{1,0:T(8,128)S(1)}, u32[]{:S(2)}, u32[]{:S(2)}) %collective-permute-start.19) | collective-permute-done | bytes 1048608 | tf_op jit(solution)/shard_map/ppermute | solution.py:39
  199.8 24.1 %collective-permute-done.20 = f32[512,512]{1,0:T(8,128)S(1)} collective-permute-done((f32[512,512]{1,0:T(8,128)S(1)}, f32[512,512]{1,0:T(8,128)S(1)}, u32[]{:S(2)}, u32[]{:S(2)}) %collective-permute-start.20) | collective-permute-done | bytes 1048608 | tf_op jit(solution)/shard_map/ppermute | solution.py:39
  225.5 2.6 collective-permute-done.21
  229.5 24.1 %collective-permute-done.22 = f32[512,512]{1,0:T(8,128)S(1)} collective-permute-done((f32[512,512]{1,0:T(8,128)S(1)}, f32[512,512]{1,0:T(8,128)S(1)}, u32[]{:S(2)}, u32[]{:S(2)}) %collective-permute-start.22) | collective-permute-done | bytes 1048608 | tf_op jit(solution)/shard_map/ppermute | solution.py:39
  254.2 24.1 %collective-permute-done.23 = f32[512,512]{1,0:T(8,128)S(1)} collective-permute-done((f32[512,512]{1,0:T(8,128)S(1)}, f32[512,512]{1,0:T(8,128)S(1)}, u32[]{:S(2)}, u32[]{:S(2)}) %collective-permute-start.23) | collective-permute-done | bytes 1048608 | tf_op jit(solution)/shard_map/ppermute | solution.py:39
  280.1 3.9 %all-to-all-start.1 = ((bf16[1,16,32,512]{3,2,0,1:T(8,128)(2,1)}), bf16[1,16,32,512]{3,2,0,1:T(8,128)(2,1)S(1)}, u32[]{:S(2)}, u32[]{:S(2)}) async-start(bf16[1,16,32,512]{3,2,0,1:T(8,128)(2,1)} %bitcast.37), calls=%async_computation.1 | async-start | bytes 1048576 | tf_op jit(solution)/shard_map/all_to_all | solution.py:124
  286.5 11.8 %all-to-all-done.1 = bf16[1,16,32,512]{3,2,0,1:T(8,128)(2,1)S(1)} async-done(((bf16[1,16,32,512]{3,2,0,1:T(8,128)(2,1)}), bf16[1,16,32,512]{3,2,0,1:T(8,128)(2,1)S(1)}, u32[]{:S(2)}, u32[]{:S(2)}) %all-to-all-start.1) | async-done | bytes 524320 | tf_op jit(solution)/shard_map/all_to_all | solution.py:124
  (90 shorter events, 33.9 us)
Async XLA Ops:
  0.7 18.8 %all-to-all-start = ((bf16[1,2,2,256,512]{4,3,2,0,1:T(8,128)(2,1)}), bf16[1,2,2,256,512]{4,3,2,0,1:T(8,128)(2,1)S(1)}, u32[]{:S(2)}, u32[]{:S(2)}) async-start(bf16[1,2,2,256,512]{4,3,2,0,1:T(8,128)(2,1)} %bitcast.94), calls=%async_computation | async-start | bytes 2097152 | tf_op jit(solution)/shard_map/all_to_all | solution.py:95
  62.5 8.1 %collective-permute-start = (bf16[1,1,32,512]{3,2,1,0:T(8,128)(2,1)S(1)}, bf16[1,1,32,512]{3,2,1,0:T(8,128)(2,1)S(1)}, u32[]{:S(2)}, u32[]{:S(2)}) collective-permute-start(bf16[1,1,32,512]{3,2,1,0:T(8,128)(2,1)S(1)} %get-tuple-element.23), channel_id=1, source_target_pairs={{0,1},{1,0},{2,3},{3,2},{4,5},{5,4},{6,7},{7,6},{8,9},{9,8},{10,11... | collective-permute-start | bytes 98312 | tf_op jit(solution)/shard_map/ppermute | solution.py:33
  62.6 53.0 %collective-permute-start.14 = (bf16[1,1,32,512]{3,2,1,0:T(8,128)(2,1)S(1)}, bf16[1,1,32,512]{3,2,1,0:T(8,128)(2,1)S(1)}, u32[]{:S(2)}, u32[]{:S(2)}) collective-permute-start(bf16[1,1,32,512]{3,2,1,0:T(8,128)(2,1)S(1)} %get-tuple-element.9), channel_id=1, source_target_pairs={{0,15},{1,14},{2,13},{3,12},{4,11},{5,10},{6,9},{7,8},{8,7},{9,6},... | collective-permute-start | bytes 98312 | tf_op jit(solution)/shard_map/ppermute | solution.py:33
  66.6 49.0 %collective-permute-start.13 = (bf16[1,1,32,512]{3,2,1,0:T(8,128)(2,1)S(1)}, bf16[1,1,32,512]{3,2,1,0:T(8,128)(2,1)S(1)}, u32[]{:S(2)}, u32[]{:S(2)}) collective-permute-start(bf16[1,1,32,512]{3,2,1,0:T(8,128)(2,1)S(1)} %get-tuple-element.10), channel_id=1, source_target_pairs={{0,14},{1,15},{2,12},{3,13},{4,10},{5,11},{6,8},{7,9},{8,6},{9,7},... | collective-permute-start | bytes 98312 | tf_op jit(solution)/shard_map/ppermute | solution.py:33
  67.4 48.2 %collective-permute-start.12 = (bf16[1,1,32,512]{3,2,1,0:T(8,128)(2,1)S(1)}, bf16[1,1,32,512]{3,2,1,0:T(8,128)(2,1)S(1)}, u32[]{:S(2)}, u32[]{:S(2)}) collective-permute-start(bf16[1,1,32,512]{3,2,1,0:T(8,128)(2,1)S(1)} %get-tuple-element.11), channel_id=1, source_target_pairs={{0,13},{1,12},{2,15},{3,14},{4,9},{5,8},{6,11},{7,10},{8,5},{9,4},... | collective-permute-start | bytes 98312 | tf_op jit(solution)/shard_map/ppermute | solution.py:33
  69.0 46.6 %collective-permute-start.11 = (bf16[1,1,32,512]{3,2,1,0:T(8,128)(2,1)S(1)}, bf16[1,1,32,512]{3,2,1,0:T(8,128)(2,1)S(1)}, u32[]{:S(2)}, u32[]{:S(2)}) collective-permute-start(bf16[1,1,32,512]{3,2,1,0:T(8,128)(2,1)S(1)} %get-tuple-element.12), channel_id=1, source_target_pairs={{0,12},{1,13},{2,14},{3,15},{4,8},{5,9},{6,10},{7,11},{8,4},{9,5},... | collective-permute-start | bytes 98312 | tf_op jit(solution)/shard_map/ppermute | solution.py:33
  70.7 4.2 %collective-permute-start.1 = (bf16[1,1,32,512]{3,2,1,0:T(8,128)(2,1)S(1)}, bf16[1,1,32,512]{3,2,1,0:T(8,128)(2,1)S(1)}, u32[]{:S(2)}, u32[]{:S(2)}) collective-permute-start(bf16[1,1,32,512]{3,2,1,0:T(8,128)(2,1)S(1)} %get-tuple-element.22), channel_id=1, source_target_pairs={{0,2},{1,3},{2,0},{3,1},{4,6},{5,7},{6,4},{7,5},{8,10},{9,11},{10,... | collective-permute-start | bytes 98312 | tf_op jit(solution)/shard_map/ppermute | solution.py:33
  74.9 3.3 %collective-permute-start.2 = (bf16[1,1,32,512]{3,2,1,0:T(8,128)(2,1)S(1)}, bf16[1,1,32,512]{3,2,1,0:T(8,128)(2,1)S(1)}, u32[]{:S(2)}, u32[]{:S(2)}) collective-permute-start(bf16[1,1,32,512]{3,2,1,0:T(8,128)(2,1)S(1)} %get-tuple-element.21), channel_id=1, source_target_pairs={{0,3},{1,2},{2,1},{3,0},{4,7},{5,6},{6,5},{7,4},{8,11},{9,10},{10,... | collective-permute-start | bytes 98312 | tf_op jit(solution)/shard_map/ppermute | solution.py:33
  78.3 3.9 %collective-permute-start.3 = (bf16[1,1,32,512]{3,2,1,0:T(8,128)(2,1)S(1)}, bf16[1,1,32,512]{3,2,1,0:T(8,128)(2,1)S(1)}, u32[]{:S(2)}, u32[]{:S(2)}) collective-permute-start(bf16[1,1,32,512]{3,2,1,0:T(8,128)(2,1)S(1)} %get-tuple-element.20), channel_id=1, source_target_pairs={{0,4},{1,5},{2,6},{3,7},{4,0},{5,1},{6,2},{7,3},{8,12},{9,13},{10,... | collective-permute-start | bytes 98312 | tf_op jit(solution)/shard_map/ppermute | solution.py:33
  82.2 3.3 %collective-permute-start.4 = (bf16[1,1,32,512]{3,2,1,0:T(8,128)(2,1)S(1)}, bf16[1,1,32,512]{3,2,1,0:T(8,128)(2,1)S(1)}, u32[]{:S(2)}, u32[]{:S(2)}) collective-permute-start(bf16[1,1,32,512]{3,2,1,0:T(8,128)(2,1)S(1)} %get-tuple-element.19), channel_id=1, source_target_pairs={{0,5},{1,4},{2,7},{3,6},{4,1},{5,0},{6,3},{7,2},{8,13},{9,12},{10,... | collective-permute-start | bytes 98312 | tf_op jit(solution)/shard_map/ppermute | solution.py:33
  85.5 4.8 %collective-permute-start.5 = (bf16[1,1,32,512]{3,2,1,0:T(8,128)(2,1)S(1)}, bf16[1,1,32,512]{3,2,1,0:T(8,128)(2,1)S(1)}, u32[]{:S(2)}, u32[]{:S(2)}) collective-permute-start(bf16[1,1,32,512]{3,2,1,0:T(8,128)(2,1)S(1)} %get-tuple-element.18), channel_id=1, source_target_pairs={{0,6},{1,7},{2,4},{3,5},{4,2},{5,3},{6,0},{7,1},{8,14},{9,15},{10,... | collective-permute-start | bytes 98312 | tf_op jit(solution)/shard_map/ppermute | solution.py:33
  90.3 4.2 %collective-permute-start.6 = (bf16[1,1,32,512]{3,2,1,0:T(8,128)(2,1)S(1)}, bf16[1,1,32,512]{3,2,1,0:T(8,128)(2,1)S(1)}, u32[]{:S(2)}, u32[]{:S(2)}) collective-permute-start(bf16[1,1,32,512]{3,2,1,0:T(8,128)(2,1)S(1)} %get-tuple-element.17), channel_id=1, source_target_pairs={{0,7},{1,6},{2,5},{3,4},{4,3},{5,2},{6,1},{7,0},{8,15},{9,14},{10,... | collective-permute-start | bytes 98312 | tf_op jit(solution)/shard_map/ppermute | solution.py:33
  94.6 5.2 %collective-permute-start.7 = (bf16[1,1,32,512]{3,2,1,0:T(8,128)(2,1)S(1)}, bf16[1,1,32,512]{3,2,1,0:T(8,128)(2,1)S(1)}, u32[]{:S(2)}, u32[]{:S(2)}) collective-permute-start(bf16[1,1,32,512]{3,2,1,0:T(8,128)(2,1)S(1)} %get-tuple-element.16), channel_id=1, source_target_pairs={{0,8},{1,9},{2,10},{3,11},{4,12},{5,13},{6,14},{7,15},{8,0},{9,1},... | collective-permute-start | bytes 98312 | tf_op jit(solution)/shard_map/ppermute | solution.py:33
  99.7 4.7 %collective-permute-start.8 = (bf16[1,1,32,512]{3,2,1,0:T(8,128)(2,1)S(1)}, bf16[1,1,32,512]{3,2,1,0:T(8,128)(2,1)S(1)}, u32[]{:S(2)}, u32[]{:S(2)}) collective-permute-start(bf16[1,1,32,512]{3,2,1,0:T(8,128)(2,1)S(1)} %get-tuple-element.15), channel_id=1, source_target_pairs={{0,9},{1,8},{2,11},{3,10},{4,13},{5,12},{6,15},{7,14},{8,1},{9,0},... | collective-permute-start | bytes 98312 | tf_op jit(solution)/shard_map/ppermute | solution.py:33
  104.4 5.7 %collective-permute-start.9 = (bf16[1,1,32,512]{3,2,1,0:T(8,128)(2,1)S(1)}, bf16[1,1,32,512]{3,2,1,0:T(8,128)(2,1)S(1)}, u32[]{:S(2)}, u32[]{:S(2)}) collective-permute-start(bf16[1,1,32,512]{3,2,1,0:T(8,128)(2,1)S(1)} %get-tuple-element.14), channel_id=1, source_target_pairs={{0,10},{1,11},{2,8},{3,9},{4,14},{5,15},{6,12},{7,13},{8,2},{9,3},... | collective-permute-start | bytes 98312 | tf_op jit(solution)/shard_map/ppermute | solution.py:33
  110.1 5.4 %collective-permute-start.10 = (bf16[1,1,32,512]{3,2,1,0:T(8,128)(2,1)S(1)}, bf16[1,1,32,512]{3,2,1,0:T(8,128)(2,1)S(1)}, u32[]{:S(2)}, u32[]{:S(2)}) collective-permute-start(bf16[1,1,32,512]{3,2,1,0:T(8,128)(2,1)S(1)} %get-tuple-element.13), channel_id=1, source_target_pairs={{0,11},{1,10},{2,9},{3,8},{4,15},{5,14},{6,13},{7,12},{8,3},{9,2},... | collective-permute-start | bytes 98312 | tf_op jit(solution)/shard_map/ppermute | solution.py:33
  116.7 2.7 collective-permute-start.15
  119.7 25.3 %collective-permute-start.16 = (f32[512,512]{1,0:T(8,128)S(1)}, f32[512,512]{1,0:T(8,128)S(1)}, u32[]{:S(2)}, u32[]{:S(2)}) collective-permute-start(f32[512,512]{1,0:T(8,128)S(1)} %add.151), channel_id=1, source_target_pairs={{0,2},{1,3},{2,0},{3,1},{4,6},{5,7},{6,4},{7,5},{8,10},{9,11},{10,... | collective-permute-start | bytes 3145736 | tf_op jit(solution)/shard_map/ppermute | solution.py:39
  145.2 24.4 %collective-permute-start.17 = (f32[512,512]{1,0:T(8,128)S(1)}, f32[512,512]{1,0:T(8,128)S(1)}, u32[]{:S(2)}, u32[]{:S(2)}) collective-permute-start(f32[512,512]{1,0:T(8,128)S(1)} %add.152), channel_id=1, source_target_pairs={{0,4},{1,5},{2,6},{3,7},{4,0},{5,1},{6,2},{7,3},{8,12},{9,13},{10,... | collective-permute-start | bytes 3145736 | tf_op jit(solution)/shard_map/ppermute | solution.py:39
  174.0 25.3 %collective-permute-start.19 = (f32[512,512]{1,0:T(8,128)S(1)}, f32[512,512]{1,0:T(8,128)S(1)}, u32[]{:S(2)}, u32[]{:S(2)}) collective-permute-start(f32[512,512]{1,0:T(8,128)S(1)} %add.156), channel_id=1, source_target_pairs={{0,2},{1,3},{2,0},{3,1},{4,6},{5,7},{6,4},{7,5},{8,10},{9,11},{10,... | collective-permute-start | bytes 3145736 | tf_op jit(solution)/shard_map/ppermute | solution.py:39
  199.5 24.4 %collective-permute-start.20 = (f32[512,512]{1,0:T(8,128)S(1)}, f32[512,512]{1,0:T(8,128)S(1)}, u32[]{:S(2)}, u32[]{:S(2)}) collective-permute-start(f32[512,512]{1,0:T(8,128)S(1)} %add.157), channel_id=1, source_target_pairs={{0,4},{1,5},{2,6},{3,7},{4,0},{5,1},{6,2},{7,3},{8,12},{9,13},{10,... | collective-permute-start | bytes 3145736 | tf_op jit(solution)/shard_map/ppermute | solution.py:39
  228.4 25.3 %collective-permute-start.22 = (f32[512,512]{1,0:T(8,128)S(1)}, f32[512,512]{1,0:T(8,128)S(1)}, u32[]{:S(2)}, u32[]{:S(2)}) collective-permute-start(f32[512,512]{1,0:T(8,128)S(1)} %add.161), channel_id=1, source_target_pairs={{0,2},{1,3},{2,0},{3,1},{4,6},{5,7},{6,4},{7,5},{8,10},{9,11},{10,... | collective-permute-start | bytes 3145736 | tf_op jit(solution)/shard_map/ppermute | solution.py:39
  253.8 24.4 %collective-permute-start.23 = (f32[512,512]{1,0:T(8,128)S(1)}, f32[512,512]{1,0:T(8,128)S(1)}, u32[]{:S(2)}, u32[]{:S(2)}) collective-permute-start(f32[512,512]{1,0:T(8,128)S(1)} %add.162), channel_id=1, source_target_pairs={{0,4},{1,5},{2,6},{3,7},{4,0},{5,1},{6,2},{7,3},{8,12},{9,13},{10,... | collective-permute-start | bytes 3145736 | tf_op jit(solution)/shard_map/ppermute | solution.py:39
  280.1 18.2 %all-to-all-start.1 = ((bf16[1,16,32,512]{3,2,0,1:T(8,128)(2,1)}), bf16[1,16,32,512]{3,2,0,1:T(8,128)(2,1)S(1)}, u32[]{:S(2)}, u32[]{:S(2)}) async-start(bf16[1,16,32,512]{3,2,0,1:T(8,128)(2,1)} %bitcast.37), calls=%async_computation.1 | async-start | bytes 1048576 | tf_op jit(solution)/shard_map/all_to_all | solution.py:124
  (5 other events, 19.6 us)
